TPU v7x, 128 devices: a whole 4x4x4 slice. The times are simulated.
128 devices in a mesh: pool: 32 (over y, x, core), head: 4 (over z).
Axes of the slice: x: 4, y: 4, z: 4, core: 2. Of those that a mesh axis runs over, the one named last changes fastest.
Arguments:
- x_rows: bfloat16 [1024, 4096], P('pool'), may hold values from -3 to 3
- query: bfloat16 [1024, 4096], P('pool', 'head'), may hold values from -170 to 170
- key_cache: bfloat16 [1024, 4, 512, 128], P('pool', 'head'), may hold values from -6 to 6
- value_cache: bfloat16 [1024, 4, 512, 128], P('pool', 'head'), may hold values from -6 to 6
- new_key: bfloat16 [1024, 512], P('pool', 'head'), may hold values from -6 to 6
- new_value: bfloat16 [1024, 512], P('pool', 'head'), may hold values from -6 to 6
- lengths: int32 [1024], P('pool'), may hold values from 2 to 512, as said below
- out_proj: bfloat16 [4096, 4096], P('head'), may hold values from -0.5 to 0.5
- norm_gain: float32 [4096], replicated, may hold values from 0.5 to 1.5
- expert_ids: int32 [1024, 8], P('pool'), may hold values from 0 to 63, all different within a row; in each aligned block of 32 rows (0 to 31, 32 to 63, ...) at most 8 rows name the same one
- gate_weights: float32 [1024, 8], P('pool'), may hold values from 0.05 to 1
- w_gate: bfloat16 [64, 4096, 1024], P('pool', None, 'head'), may hold values from -0.09375 to 0.09375
- w_up: bfloat16 [64, 4096, 1024], P('pool', None, 'head'), may hold values from -0.09375 to 0.09375
- w_down: bfloat16 [64, 1024, 4096], P('pool', 'head'), may hold values from -0.1875 to 0.1875
Outputs:
- layer_out: bfloat16 [1024, 4096], P('pool', 'head')
Inputs may be any that keep to these rules, and one draw needn't show every extreme that they name: `expert_ids`: within the 32 requests of one index of pool, no expert is named by more than 8 pairs, a bound that some block reaches. `lengths`: request 0 uses all 512 slots.
All inputs are finite; a program needn't handle non-finite values.
Results may differ from a plain program's by a relative error of at most 0.017.
Values may be sent and summed in bfloat16 or wider, within the bound.
No kernel may reach another device: no remote copies, remote signals or barrier semaphores. Data moves between devices by JAX's collectives and lax.ppermute only.
A program may use at most 128 MiB of HBM per device.

v0:
```python
import jax
import jax.numpy as jnp
from jax import lax
from jax.sharding import PartitionSpec as P


def attend(query, key_cache, value_cache, new_key, new_value, lengths):
    token_count = query.shape[0]
    head_size = new_key.shape[1]
    queries = query.reshape(token_count, -1, head_size)
    cached_keys = key_cache[:, 0]
    cached_values = value_cache[:, 0]
    score_scale = head_size ** (-0.5)
    scores = (
        jnp.einsum("rqd,rcd->rqc", queries, cached_keys, preferred_element_type=jnp.float32)
        * score_scale
    )
    fresh_score = (
        jnp.einsum("rqd,rd->rq", queries, new_key, preferred_element_type=jnp.float32) * score_scale
    )
    live_mask = (jnp.arange(cached_keys.shape[1])[None, :] < lengths[:, None])[:, None, :]
    scores = jnp.where(live_mask, scores, -1e30)
    highest = jnp.maximum(jnp.max(scores, -1), fresh_score)
    weights = jnp.where(live_mask, jnp.exp(scores - highest[..., None]), 0.0)
    own_term = jnp.exp(fresh_score - highest)
    totals = jnp.sum(weights, -1) + own_term
    probs = (weights / totals[..., None]).astype(jnp.bfloat16)
    own_prob = (own_term / totals).astype(jnp.bfloat16)
    mixed = jnp.einsum("rqc,rcd->rqd", probs, cached_values, preferred_element_type=jnp.float32)
    mixed = (
        mixed + own_prob.astype(jnp.float32)[..., None] * new_value.astype(jnp.float32)[:, None, :]
    )
    return mixed.astype(jnp.bfloat16).reshape(token_count, -1)


def route_tables(expert_ids, gate_weights, experts, capacity):
    token_count, choose = expert_ids.shape
    flat_ids = expert_ids.reshape(-1)
    one_hot = (flat_ids[:, None] == jnp.arange(experts)[None, :]).astype(jnp.int32)
    earlier = jnp.cumsum(one_hot, 0) - one_hot
    ranking = jnp.sum(earlier * one_hot, 1)
    slot_index = flat_ids * capacity + ranking
    matching = (jnp.arange(experts * capacity)[:, None] == slot_index[None, :]).reshape(
        experts * capacity, token_count, choose
    )
    send_table = jnp.sum(matching.astype(jnp.float32), 2).astype(jnp.bfloat16)
    take_table = jnp.sum(jnp.where(matching, gate_weights[None, :, :], 0.0), 2).T
    return (send_table, take_table)


def experts_apply(arrived, w_gate, w_up, w_down):
    gate_part = jnp.einsum("secd,edf->secf", arrived, w_gate, preferred_element_type=jnp.float32)
    up_part = jnp.einsum("secd,edf->secf", arrived, w_up, preferred_element_type=jnp.float32)
    act = (jax.nn.silu(gate_part) * up_part).astype(jnp.bfloat16)
    return jnp.einsum("secf,efd->secd", act, w_down, preferred_element_type=jnp.float32)


def body(
    x_rows,
    query,
    key_cache,
    value_cache,
    new_key,
    new_value,
    lengths,
    out_proj,
    norm_gain,
    expert_ids,
    gate_weights,
    w_gate,
    w_up,
    w_down,
):
    pools = lax.axis_size("pool")
    groups = lax.axis_size("head")
    width = x_rows.shape[1]
    share = width // groups
    local_experts = w_gate.shape[0]
    all_experts = pools * local_experts
    capacity = max(2, 2 * expert_ids.shape[0] * expert_ids.shape[1] // all_experts)
    attn = attend(query, key_cache, value_cache, new_key, new_value, lengths)
    partial_value = jnp.dot(attn, out_proj, preferred_element_type=jnp.float32)
    send_table, take_table = route_tables(expert_ids, gate_weights, all_experts, capacity)
    offset = lax.axis_index("head") * share
    hidden = x_rows.astype(jnp.float32) + lax.psum(
        partial_value.astype(jnp.bfloat16), "head"
    ).astype(jnp.float32)
    mean_square = jnp.mean(hidden * hidden, -1, keepdims=True)
    normed = (hidden * lax.rsqrt(mean_square + 1e-06) * norm_gain[None, :]).astype(jnp.bfloat16)
    outgoing = (
        jnp.dot(send_table, normed, preferred_element_type=jnp.float32)
        .astype(jnp.bfloat16)
        .reshape(pools, -1, width)
    )
    arrived = lax.all_to_all(outgoing, "pool", split_axis=0, concat_axis=0, tiled=True)
    produced = experts_apply(
        arrived.reshape(pools, local_experts, capacity, width), w_gate, w_up, w_down
    )
    produced = lax.psum(produced.astype(jnp.bfloat16), "head")
    returned = lax.all_to_all(
        produced.reshape(pools, -1, width), "pool", split_axis=0, concat_axis=0, tiled=True
    )
    moe_sum = jnp.dot(
        take_table, returned.reshape(-1, width).astype(jnp.float32), precision=lax.Precision.HIGHEST
    )
    finished = hidden + moe_sum
    return lax.dynamic_slice_in_dim(finished, offset, share, 1).astype(jnp.bfloat16)


def solution(mesh):
    placed = (
        P("pool", None),
        P("pool", "head"),
        P("pool", "head", None, None),
        P("pool", "head", None, None),
        P("pool", "head"),
        P("pool", "head"),
        P("pool"),
        P("head", None),
        P(),
        P("pool", None),
        P("pool", None),
        P("pool", None, "head"),
        P("pool", None, "head"),
        P("pool", "head", None),
    )
    return jax.shard_map(
        body, mesh=mesh, in_specs=placed, out_specs=P("pool", "head"), check_vma=False
    )
```

profile of v0, /device:TPU:0, one launch (start us, length us, event | category | flops | bytes accessed | tf_op | source)
XLA Modules:
  0.0 304.0 jit_solution(16278272541698673287)
XLA Ops:
  6.5 0.9 copy.38
  7.4 0.7 iota_compare_fusion.3
  8.2 0.1 fusion.69
  8.3 3.6 %fusion.75 = (f32[32,8]{1,0:T(8,128)S(1)}, f32[32,8,512]{2,1,0:T(8,128)S(1)}) fusion(bf16[32,8,128]{2,1,0:T(8,128)(2,1)S(1)} %bitcast.105, bf16[32,1,512,128]{3,2,1,0:T(8,128)(2,1)} %param.16, pred[32,512]{1,0:T(8,128)(4,1)S(1)} %iota_compare_fusion.3), kind=kOutput, calls=%fused_computation.71 | convolution fusion | flops 33947392 | bytes 4801536 | tf_op jit(solution)/shard_map/rqd,rcd->rqc/dot_general | solution.py:15
  11.9 0.3 fusion.53
  12.3 2.9 fusion.45
  15.2 2.3 convolution_convert_fusion.2
  17.5 0.0 all-reduce.3.cloned.1.call-update
  17.5 0.0 all-reduce.5.cloned.1.call-start
  17.6 0.1 copy.24
  17.7 0.1 eq.40
  17.7 0.1 eq.44
  17.8 0.6 reduce-window.6
  18.5 0.2 slice_reduce_fusion
  18.7 0.1 fusion.66
  18.8 0.1 reduce_sum.49
  18.9 0.1 copy.28
  19.0 0.4 convert_reduce_fusion
  19.4 42.9 %all-reduce.3.cloned.1.call-done = bf16[32,4096]{1,0:T(8,128)(2,1)} async-done(((bf16[32,4096]{1,0:T(8,128)(2,1)}), bf16[32,4096]{1,0:T(8,128)(2,1)}) %all-reduce.3.cloned.1.call-update) | async-done | bytes 262160 | tf_op jit(solution)/shard_map/psum | solution.py:85
  62.3 1.2 convert_add_fusion
  63.5 2.3 convolution_convert_fusion.1
  65.7 58.1 %all_to_all.10 = bf16[32,16,4096]{2,1,0:T(8,128)(2,1)S(1)} all-to-all(bf16[32,16,4096]{2,1,0:T(8,128)(2,1)S(1)} %bitcast.102), channel_id=1, replica_groups=mesh['pool'=32,'head'=4] {'pool'}, dimensions={0} | all-to-all | bytes 8388608 | tf_op jit(solution)/shard_map/all_to_all | solution.py:95
  123.8 2.0 copy-done.2
  125.8 1.2 fusion.18
  127.0 9.0 %fusion = bf16[32,2,8,4096]{3,2,0,1:T(8,128)(2,1)} fusion(bf16[2,256,4096]{2,1,0:T(8,128)(2,1)} %param.27, bf16[2,4096,256]{2,1,0:T(8,128)(2,1)} %param.26, f32[32,2,8,256]{3,2,0,1:T(8,128)S(1)} %fusion.18, bf16[32,16,4096]{2,1,0:T(8,128)(2,1)} %copy-done.2), kind=kOutput, calls=%fused_computation.2 | convolution fusion | flops 2150367232 | bytes 17301504 | tf_op jit(solution)/shard_map/secf,efd->secd/dot_general | solution.py:55
  136.1 4.7 %copy.62 = bf16[32,2,8,4096]{3,2,1,0:T(8,128)(2,1)} copy(bf16[32,2,8,4096]{3,2,0,1:T(8,128)(2,1)} %fusion) | data formatting | bytes 8388608 | tf_op jit(solution)/shard_map/convert_element_type | solution.py:99
  140.7 0.0 all-reduce.5.cloned.1.call-update
  140.7 90.2 %all-reduce.5.cloned.1.call-done = bf16[32,16,4096]{2,1,0:T(8,128)(2,1)} async-done(((bf16[32,16,4096]{2,1,0:T(8,128)(2,1)}), bf16[32,16,4096]{2,1,0:T(8,128)(2,1)}) %all-reduce.5.cloned.1.call-update) | async-done | bytes 4194320 | tf_op jit(solution)/shard_map/psum | solution.py:99
  230.9 7.2 %all-to-all-start.1 = ((bf16[32,16,4096]{2,1,0:T(8,128)(2,1)}), bf16[32,16,4096]{2,1,0:T(8,128)(2,1)}, u32[]{:S(2)}, u32[]{:S(2)}) async-start(bf16[32,16,4096]{2,1,0:T(8,128)(2,1)} %all-reduce.5.cloned.1.call-done), calls=%async_computation.1 | async-start | bytes 8388608 | tf_op jit(solution)/shard_map/all_to_all | solution.py:100
  238.2 54.0 %all-to-all-done.1 = bf16[32,16,4096]{2,1,0:T(8,128)(2,1)} async-done(((bf16[32,16,4096]{2,1,0:T(8,128)(2,1)}), bf16[32,16,4096]{2,1,0:T(8,128)(2,1)}, u32[]{:S(2)}, u32[]{:S(2)}) %all-to-all-start.1) | async-done | bytes 4194336 | tf_op jit(solution)/shard_map/all_to_all | solution.py:100
  292.1 4.3 %fusion.76 = f32[32,4096]{1,0:T(8,128)S(1)} fusion(f32[512,32]{0,1:T(8,128)S(1)} %get-tuple-element.6, bf16[512,4096]{1,0:T(8,128)(2,1)} %bitcast.18), kind=kOutput, calls=%fused_computation.72 | convolution fusion | flops 805306368 | bytes 4784128 | tf_op jit(solution)/shard_map/dot_general | solution.py:103
  296.5 0.7 fusion.61
  (26 shorter events, 0.1 us)
Async XLA Ops:
  6.5 1.6 copy-start
  6.5 5.7 %copy-start.5 = (bf16[32,128]{1,0:T(8,128)(2,1)S(1)}, bf16[32,128]{1,0:T(8,128)(2,1)}, u32[]{:S(2)}) copy-start(bf16[32,128]{1,0:T(8,128)(2,1)} %param.19) | copy-start | bytes 24580
  6.5 55.7 %all-reduce.3.cloned.1.call-start = ((), (), s32[]{:S(2)}) async-start(), calls=%async_computation.2 | async-start | bytes 524288 | tf_op jit(solution)/shard_map/psum | solution.py:85
  8.3 6.9 %copy-start.1 = (bf16[1024,4096]{1,0:T(8,128)(2,1)S(1)}, bf16[1024,4096]{1,0:T(8,128)(2,1)}, u32[]{:S(2)}) copy-start(bf16[1024,4096]{1,0:T(8,128)(2,1)} %param.21) | copy-start | bytes 25165828
  15.2 2.4 copy-start.6
  15.2 3.7 %copy-start.7 = (f32[32,8]{0,1:T(8,128)S(1)}, f32[32,8]{0,1:T(8,128)}, u32[]{:S(2)}) copy-start(f32[32,8]{0,1:T(8,128)} %param.24) | copy-start | bytes 3076
  15.2 47.1 %copy-start.3 = (bf16[32,4096]{1,0:T(8,128)(2,1)S(1)}, bf16[32,4096]{1,0:T(8,128)(2,1)}, u32[]{:S(2)}) copy-start(bf16[32,4096]{1,0:T(8,128)(2,1)} %param.14) | copy-start | bytes 786436
  15.2 48.2 %copy-start.4 = (f32[4096]{0:T(1024)S(1)}, f32[4096]{0:T(1024)}, u32[]{:S(2)}) copy-start(f32[4096]{0:T(1024)} %param.22) | copy-start | bytes 49156
  17.5 213.4 %all-reduce.5.cloned.1.call-start = ((), (), s32[]{:S(2)}) async-start(), calls=%async_computation.3 | async-start | bytes 8388608 | tf_op jit(solution)/shard_map/psum | solution.py:99
  65.7 60.1 %copy-start.8 = (bf16[2,4096,256]{2,1,0:T(8,128)(2,1)S(1)}, bf16[2,4096,256]{2,1,0:T(8,128)(2,1)}, u32[]{:S(2)}) copy-start(bf16[2,4096,256]{2,1,0:T(8,128)(2,1)} %param.25) | copy-start | bytes 12582916
  123.8 2.0 copy-start.2
  230.9 61.2 %all-to-all-start.1 = ((bf16[32,16,4096]{2,1,0:T(8,128)(2,1)}), bf16[32,16,4096]{2,1,0:T(8,128)(2,1)}, u32[]{:S(2)}, u32[]{:S(2)}) async-start(bf16[32,16,4096]{2,1,0:T(8,128)(2,1)} %all-reduce.5.cloned.1.call-done), calls=%async_computation.1 | async-start | bytes 8388608 | tf_op jit(solution)/shard_map/all_to_all | solution.py:100
Sparse Core Ops, SparseCore 0:
  17.6 44.6 all-reduce.2
  140.9 90.0 all-reduce.4
where the time goes:
time: 304 us
  waiting for transfers between devices  187 us (62%)
  blocking collectives  58.1 us (19%)
  matrix products  25.8 us (8%)
  between operations  13.6 us (4%)
  local copies, waits for them, and re-layouts  8.15 us (3%)
  starting transfers between devices  7.27 us (2%)
  other arithmetic  4.02 us (1%)
    psum x1, waiting for transfers between devices, body(): produced = lax.psum(produced.astype(jnp.bfloat16), 'head')  90.2 us
    all_to_all x1, blocking collectives, body(): lax.all_to_all(outgoing, 'pool', split_axis=0, concat_axis=0, tiled=True)  58.1 us
    all_to_all x1, waiting for transfers between devices, body(): lax.all_to_all(produced.reshape(pools, -1, width), 'pool', split_axis=0,...  54 us
    psum x1, waiting for transfers between devices, body(): lax.psum(partial_value.astype(jnp.bfloat16), 'head').astype(jnp.float32)  42.9 us
    dot_general x1, matrix products, experts_apply(): jnp.einsum('secf,efd->secd', act, w_down, preferred_element_type=jnp.floa...  9.02 us
    all_to_all x1, starting transfers between devices, body(): lax.all_to_all(produced.reshape(pools, -1, width), 'pool', split_axis=0,...  7.22 us
  transfers between devices with their start and end apart: 3, of which 3 were waited for; matrix products, arithmetic and copies ran while one was open for 1% of the time, Pallas kernels for 0%

commit v1 on v0

v1 whole, which is shorter than its diff:
```python
import jax
import jax.numpy as jnp
from jax import lax
from jax.sharding import PartitionSpec as P

F32 = jnp.float32
BF16 = jnp.bfloat16


def attend(query, key_cache, value_cache, new_key, new_value, lengths):
    token_count = query.shape[0]
    head_size = new_key.shape[1]
    queries = query.reshape(token_count, -1, head_size)
    cached_keys = key_cache[:, 0]
    cached_values = value_cache[:, 0]
    score_scale = head_size ** (-0.5)
    scores = (
        jnp.einsum("rqd,rcd->rqc", queries, cached_keys, preferred_element_type=jnp.float32)
        * score_scale
    )
    fresh_score = (
        jnp.einsum("rqd,rd->rq", queries, new_key, preferred_element_type=jnp.float32) * score_scale
    )
    live_mask = (jnp.arange(cached_keys.shape[1])[None, :] < lengths[:, None])[:, None, :]
    scores = jnp.where(live_mask, scores, -1e30)
    highest = jnp.maximum(jnp.max(scores, -1), fresh_score)
    weights = jnp.where(live_mask, jnp.exp(scores - highest[..., None]), 0.0)
    own_term = jnp.exp(fresh_score - highest)
    totals = jnp.sum(weights, -1) + own_term
    probs = (weights / totals[..., None]).astype(jnp.bfloat16)
    own_prob = (own_term / totals).astype(jnp.bfloat16)
    mixed = jnp.einsum("rqc,rcd->rqd", probs, cached_values, preferred_element_type=jnp.float32)
    mixed = (
        mixed + own_prob.astype(jnp.float32)[..., None] * new_value.astype(jnp.float32)[:, None, :]
    )
    return mixed.astype(jnp.bfloat16).reshape(token_count, -1)


def route_slots(expert_ids, capacity):
    flat = expert_ids.reshape(-1)
    count = flat.shape[0]
    order = jnp.arange(count)
    earlier = (flat[:, None] == flat[None, :]) & (order[None, :] < order[:, None])
    rank = jnp.sum(earlier.astype(jnp.int32), 1)
    return (flat * capacity + rank).reshape(expert_ids.shape)


def head_scatter_sum(terms, groups):
    share = terms.shape[1] // groups
    me = lax.axis_index("head")
    total = lax.dynamic_slice_in_dim(terms, me * share, share, 1)
    total = total.astype(F32)
    rounded = terms.astype(BF16)
    for step in range(1, groups):
        to = lax.rem(me + step, groups)
        piece = lax.dynamic_slice_in_dim(rounded, to * share, share, 1)
        got = lax.ppermute(piece, "head", [(i, (i + step) % groups) for i in range(groups)])
        total = total + got.astype(F32)
    return total


def body(
    x_rows,
    query,
    key_cache,
    value_cache,
    new_key,
    new_value,
    lengths,
    out_proj,
    norm_gain,
    expert_ids,
    gate_weights,
    w_gate,
    w_up,
    w_down,
):
    pools = lax.axis_size("pool")
    groups = lax.axis_size("head")
    rows, width = x_rows.shape
    share = width // groups
    local_experts = w_gate.shape[0]
    hidden_units = w_gate.shape[2]
    all_experts = pools * local_experts
    capacity = max(2, 2 * expert_ids.shape[0] * expert_ids.shape[1] // all_experts)
    slots = local_experts * capacity
    offset = lax.axis_index("head") * share

    attn = attend(query, key_cache, value_cache, new_key, new_value, lengths)
    terms = jnp.dot(attn, out_proj, preferred_element_type=F32)

    slot = route_slots(expert_ids, capacity)
    matching = jnp.arange(pools * slots)[:, None, None] == slot[None, :, :]
    send_table = jnp.sum(matching.astype(F32), 2).astype(BF16)
    take = jnp.sum(jnp.where(matching, gate_weights[None, :, :], 0.0), 2).T

    summed = head_scatter_sum(terms, groups)
    hidden = lax.dynamic_slice_in_dim(x_rows, offset, share, 1).astype(F32) + summed
    gain = lax.dynamic_slice_in_dim(norm_gain, offset, share, 0)
    scaled = (hidden * gain[None, :]).astype(BF16)
    outgoing = jnp.dot(send_table, scaled, preferred_element_type=F32).astype(BF16)
    outgoing = jnp.broadcast_to(
        outgoing.reshape(pools, 1, slots, share), (pools, groups, slots, share)
    ).reshape(pools * groups, slots, share)
    arrived = lax.all_to_all(outgoing, ("pool", "head"), split_axis=0, concat_axis=0, tiled=True)
    arrived = arrived.reshape(pools, groups, local_experts, capacity, share)

    gain_parts = norm_gain.reshape(groups, share)
    plain = arrived.astype(F32) / gain_parts[None, :, None, None, :]
    mean_square = jnp.sum(plain * plain, (1, 4)) / width
    inverse = lax.rsqrt(mean_square + 1e-06)
    inverse = inverse.transpose(1, 0, 2).reshape(local_experts, pools * capacity, 1)
    picked = arrived.transpose(2, 0, 3, 1, 4).reshape(local_experts, pools * capacity, width)
    gate_part = jnp.einsum("end,edf->enf", picked, w_gate, preferred_element_type=F32) * inverse
    up_part = jnp.einsum("end,edf->enf", picked, w_up, preferred_element_type=F32) * inverse
    act = (jax.nn.silu(gate_part) * up_part).astype(BF16)
    produced = jnp.einsum("enf,efd->end", act, w_down, preferred_element_type=F32).astype(BF16)
    produced = produced.reshape(local_experts, pools, capacity, groups, share)
    produced = produced.transpose(1, 3, 0, 2, 4).reshape(pools * groups, slots, share)
    returned = lax.all_to_all(produced, ("pool", "head"), split_axis=0, concat_axis=0, tiled=True)
    returned = returned.reshape(pools * groups * slots, share)
    take_all = jnp.broadcast_to(
        take.reshape(rows, pools, 1, slots), (rows, pools, groups, slots)
    ).reshape(rows, -1)
    take_high = take_all.astype(BF16)
    take_low = (take_all - take_high.astype(F32)).astype(BF16)
    moe = jnp.dot(take_high, returned, preferred_element_type=F32) + jnp.dot(
        take_low, returned, preferred_element_type=F32
    )
    return (hidden + moe).astype(BF16)


def solution(mesh):
    placed = (
        P("pool", None),
        P("pool", "head"),
        P("pool", "head", None, None),
        P("pool", "head", None, None),
        P("pool", "head"),
        P("pool", "head"),
        P("pool"),
        P("head", None),
        P(),
        P("pool", None),
        P("pool", None),
        P("pool", None, "head"),
        P("pool", None, "head"),
        P("pool", "head", None),
    )
    return jax.shard_map(
        body, mesh=mesh, in_specs=placed, out_specs=P("pool", "head"), check_vma=False
    )
```

time: 304 us -> 182 us (0.60)
  waiting for transfers between devices: 187 us -> 105 us
  blocking collectives: 58.1 us -> 0 us
  starting transfers between devices: 7.27 us -> 22.4 us
  between operations: 13.6 us -> 0.25 us
  matrix products: 25.8 us -> 32.5 us
  local copies, waits for them, and re-layouts: 8.15 us -> 14.4 us
    psum x2 -> x0, waiting for transfers between devices: 133 us -> none  [the longest x1 90.2 us: body(): produced = lax.psum(produced.astype(jnp.bfloat16), 'head')]
    all_to_all x1 -> x0, blocking collectives: 58.1 us -> none  [body(): lax.all_to_all(outgoing, 'pool', split_axis=0, concat_axis=0, tiled=True)]
    all_to_all x1 -> x2, waiting for transfers between devices: 54 us -> 102 us  [the longest x1 51.2 us: body(): lax.all_to_all(produced, ('pool', 'head'), split_axis=0, concat_axis=0, t...]
    all_to_all x1 -> x2, starting transfers between devices: 7.22 us -> 15.7 us  [the longest x1 9.78 us: body(): lax.all_to_all(outgoing, ('pool', 'head'), split_axis=0, concat_axis=0, t...]
    dot_general x5 -> x6, matrix products: 19.1 us -> 25.9 us  [the longest x1 9.07 us: body(): jnp.einsum('enf,efd->end', act, w_down, preferred_element_type=F32)]
    ppermute x0 -> x3, starting transfers between devices: none -> 6.69 us  [head_scatter_sum(): lax.ppermute(piece, 'head', [(i, (i + step) % groups) for i in range(grou...]
    transpose x0 -> x2, local copies, waits for them, and re-layouts: none -> 4.92 us  [the longest x1 4.8 us: body(): arrived.transpose(2, 0, 3, 1, 4)]
    reshape x0 -> x1, local copies, waits for them, and re-layouts: none -> 4.84 us  [body(): produced = produced.reshape(local_experts, pools, capacity, groups, share)]
  transfers between devices with their start and end apart: 3 -> 5, of which waited for: 3 -> 4; matrix products, arithmetic and copies ran while one was open for 1% -> 1% of each run, Pallas kernels for 0% -> 0%
where the time goes in v1:
time: 182 us; the launch traced here: 180 us
  waiting for transfers between devices  105 us (58%)
  matrix products  32.5 us (18%)
  starting transfers between devices  22.4 us (12%)
  local copies, waits for them, and re-layouts  14.4 us (8%)
  other arithmetic  5.71 us (3%)
    all_to_all x1, waiting for transfers between devices, body(): lax.all_to_all(produced, ('pool', 'head'), split_axis=0, concat_axis=0, t...  51.2 us
    all_to_all x1, waiting for transfers between devices, body(): lax.all_to_all(outgoing, ('pool', 'head'), split_axis=0, concat_axis=0, t...  51.1 us
    all_to_all x1, starting transfers between devices, body(): lax.all_to_all(outgoing, ('pool', 'head'), split_axis=0, concat_axis=0, t...  9.78 us
    dot_general x1, matrix products, body(): jnp.einsum('enf,efd->end', act, w_down, preferred_element_type=F32)  9.07 us
    ppermute x3, starting transfers between devices, head_scatter_sum(): lax.ppermute(piece, 'head', [(i, (i + step) % groups) for i in range(grou...  6.69 us
    all_to_all x1, starting transfers between devices, body(): lax.all_to_all(produced, ('pool', 'head'), split_axis=0, concat_axis=0, t...  5.91 us
    dot_general x1, matrix products, body(): terms = jnp.dot(attn, out_proj, preferred_element_type=F32)  4.94 us
    reshape x1, local copies, waits for them, and re-layouts, body(): produced = produced.reshape(local_experts, pools, capacity, groups, share)  4.84 us
  transfers between devices with their start and end apart: 5, of which 4 were waited for; matrix products, arithmetic and copies ran while one was open for 1% of the time, Pallas kernels for 0%

profile of v1, /device:TPU:0, one launch (start us, length us, event | category | flops | bytes accessed | tf_op | source)
XLA Modules:
  0.0 179.8 jit_solution(11612482870401116717)
XLA Ops:
  0.0 0.8 iota_compare_fusion.2
  0.8 0.9 copy.55
  1.6 0.1 fusion.38
  1.8 3.5 %fusion.44 = (f32[32,8]{1,0:T(8,128)S(1)}, f32[32,8,512]{2,1,0:T(8,128)S(1)}) fusion(bf16[32,8,128]{2,1,0:T(8,128)(2,1)S(1)} %bitcast.69, bf16[32,1,512,128]{3,2,1,0:T(8,128)(2,1)} %param.16, pred[32,512]{1,0:T(8,128)(4,1)S(1)} %iota_compare_fusion.2), kind=kOutput, calls=%fused_computation.61 | convolution fusion | flops 33947392 | bytes 4801536 | tf_op jit(solution)/shard_map/rqd,rcd->rqc/dot_general | solution.py:18
  5.3 0.3 fusion.25
  5.6 2.9 %fusion.17 = bf16[32,8,128]{2,1,0:T(8,128)(2,1)S(1)} fusion(bf16[32,1,512,128]{3,2,1,0:T(8,128)(2,1)} %param.17, f32[32,8,512]{2,1,0:T(8,128)S(1)} %get-tuple-element.15, f32[32,8]{1,0:T(8,128)S(1)} %get-tuple-element.13, f32[32,8]{1,0:T(8,128)S(1)} %multiply_maximum_fusion, pred[32,512]{1,0:T(8,128)(4,1)S(1)} %iota_compare_fusion.2, ...), kind=kOutput, calls=%fused_computation.17 | convolution fusion | flops 34177024 | bytes 4819968 | tf_op jit(solution)/shard_map/rqc,rcd->rqd/dot_general | solution.py:32
  8.6 4.9 %fusion.45 = (bf16[32,4096]{1,0:T(8,128)(2,1)S(1)}, f32[32,4096]{1,0:T(8,128)S(1)}) fusion(bf16[1024,4096]{1,0:T(8,128)(2,1)} %param.21, bf16[4,8,8,128]{3,2,1,0:T(8,128)(2,1)S(1)} %bitcast.67), kind=kOutput, calls=%fused_computation.62 | convolution fusion | flops 268566528 | bytes 9240576 | tf_op jit(solution)/shard_map/dot_general | solution.py:90
  13.5 2.1 %collective-permute-start = (bf16[32,1024]{1,0:T(8,128)(2,1)S(1)}, bf16[32,1024]{1,0:T(8,128)(2,1)S(1)}, u32[]{:S(2)}, u32[]{:S(2)}) collective-permute-start(bf16[32,1024]{1,0:T(8,128)(2,1)S(1)} %get-tuple-element.9), channel_id=1, source_target_pairs={{0,1},{1,2},{2,3},{3,0},{4,5},{5,6},{6,7},{7,4},{8,9},{9,10},{10,1... | collective-permute-start | bytes 196616 | tf_op jit(solution)/shard_map/ppermute | solution.py:57
  15.6 3.6 %collective-permute-start.1 = (bf16[32,1024]{1,0:T(8,128)(2,1)S(1)}, bf16[32,1024]{1,0:T(8,128)(2,1)S(1)}, u32[]{:S(2)}, u32[]{:S(2)}) collective-permute-start(bf16[32,1024]{1,0:T(8,128)(2,1)S(1)} %get-tuple-element.11), channel_id=1, source_target_pairs={{0,2},{1,3},{2,0},{3,1},{4,6},{5,7},{6,4},{7,5},{8,10},{9,11},{10,... | collective-permute-start | bytes 196616 | tf_op jit(solution)/shard_map/ppermute | solution.py:57
  19.2 1.0 collective-permute-start.2
  20.4 0.2 convert_reduce_fusion.1
  20.8 0.4 convert_reduce_fusion
  21.2 1.2 collective-permute-done.1
  22.4 1.1 collective-permute-done.2
  23.5 0.9 add_add_fusion
  24.4 0.4 convolution_convert_fusion.1
  24.8 2.6 %broadcast_in_dim.66 = bf16[32,4,16,1024]{3,2,1,0:T(8,128)(2,1)} broadcast(bf16[32,16,1024]{2,1,0:T(8,128)(2,1)S(1)} %bitcast.63), dimensions={0,2,3} | broadcast | bytes 5242880 | tf_op jit(solution)/shard_map/broadcast_in_dim | solution.py:102
  27.4 9.8 %all-to-all-start = ((bf16[128,16,1024]{2,1,0:T(8,128)(2,1)}), bf16[128,16,1024]{2,1,0:T(8,128)(2,1)}, u32[]{:S(2)}, u32[]{:S(2)}) async-start(bf16[128,16,1024]{2,1,0:T(8,128)(2,1)} %bitcast.61), calls=%async_computation | async-start | bytes 8388608 | tf_op jit(solution)/shard_map/all_to_all | solution.py:105
  37.2 0.1 div.40
  37.3 0.2 div.41
  37.5 51.1 %all-to-all-done = bf16[128,16,1024]{2,1,0:T(8,128)(2,1)} async-done(((bf16[128,16,1024]{2,1,0:T(8,128)(2,1)}), bf16[128,16,1024]{2,1,0:T(8,128)(2,1)}, u32[]{:S(2)}, u32[]{:S(2)}) %all-to-all-start) | async-done | bytes 4194336 | tf_op jit(solution)/shard_map/all_to_all | solution.py:105
  88.6 4.8 %copy.49 = bf16[2,32,8,4,1024]{4,2,3,1,0:T(8,128)(2,1)} copy(bf16[2,32,8,4,1024]{4,2,0,3,1:T(8,128)(2,1)} %bitcast.11) | data formatting | bytes 8388608 | tf_op jit(solution)/shard_map/transpose | solution.py:113
  93.4 3.0 %multiply_reduce_fusion = f32[128,16]{1,0:T(8,128)S(1)} fusion(bf16[128,16,1024]{2,1,0:T(8,128)(2,1)} %all-to-all-done, f32[128,1024]{1,0:T(8,128)S(1)} %div.41), kind=kLoop, calls=%fused_computation | loop fusion | flops 8386560 | bytes 4726784 | tf_op jit(solution)/shard_map/reduce_sum | solution.py:110
  96.4 0.1 reduce_sum.60
  96.9 4.7 %convolution_multiply_fusion.1 = f32[2,256,256]{2,1,0:T(8,128)S(1)} fusion(bf16[2,256,4096]{2,1,0:T(8,128)(2,1)} %bitcast.58, bf16[2,4096,256]{2,1,0:T(8,128)(2,1)} %param.25, f32[2,256]{1,0:T(2,128)S(1)} %mul.97), kind=kOutput, calls=%fused_computation.8 | convolution fusion | flops 1073872896 | bytes 8914944 | tf_op jit(solution)/shard_map/end,edf->enf/dot_general | solution.py:114
  101.6 9.1 %convolution_convert_fusion = bf16[2,256,4096]{2,1,0:T(8,128)(2,1)} fusion(bf16[2,256,4096]{2,1,0:T(8,128)(2,1)} %param.27, bf16[2,256,4096]{2,1,0:T(8,128)(2,1)} %bitcast.59, bf16[2,4096,256]{2,1,0:T(8,128)(2,1)} %param.26, f32[2,256,256]{2,1,0:T(8,128)S(1)} %convolution_multiply_fusion.1, f32[2,256]{1,0:T(2,128)S(1)} %mul.97), kind=kOutput, calls=%fused_computation.1 | convolution fusion | flops 2150498304 | bytes 17303552 | tf_op jit(solution)/shard_map/enf,efd->end/dot_general | solution.py:117
  110.7 4.8 %copy.52 = bf16[2,32,8,4,1024]{4,2,0,3,1:T(8,128)(2,1)} copy(bf16[2,32,8,4,1024]{4,2,3,1,0:T(8,128)(2,1)} %bitcast.60) | data formatting | bytes 8388608 | tf_op jit(solution)/shard_map/reshape | solution.py:118
  115.6 5.9 %all-to-all-start.1 = ((bf16[128,16,1024]{2,1,0:T(8,128)(2,1)}), bf16[128,16,1024]{2,1,0:T(8,128)(2,1)}, u32[]{:S(2)}, u32[]{:S(2)}) async-start(bf16[128,16,1024]{2,1,0:T(8,128)(2,1)} %bitcast.62), calls=%async_computation.1 | async-start | bytes 8388608 | tf_op jit(solution)/shard_map/all_to_all | solution.py:120
  121.5 0.1 copy.48
  121.7 51.2 %all-to-all-done.1 = bf16[128,16,1024]{2,1,0:T(8,128)(2,1)} async-done(((bf16[128,16,1024]{2,1,0:T(8,128)(2,1)}), bf16[128,16,1024]{2,1,0:T(8,128)(2,1)}, u32[]{:S(2)}, u32[]{:S(2)}) %all-to-all-start.1) | async-done | bytes 4194336 | tf_op jit(solution)/shard_map/all_to_all | solution.py:120
  172.9 3.0 %fusion.46 = f32[32,1024]{1,0:T(8,128)S(1)} fusion(bf16[32,2048]{0,1:T(8,128)(2,1)S(1)} %bitcast.65, bf16[2048,1024]{1,0:T(8,128)(2,1)} %bitcast.17), kind=kOutput, calls=%fused_computation.63 | convolution fusion | flops 134217728 | bytes 4456448 | tf_op jit(solution)/shard_map/dot_general | solution.py:127
  176.1 3.7 %fusion.16 = bf16[32,1024]{1,0:T(8,128)(2,1)} fusion(f32[32,1024]{1,0:T(8,128)S(1)} %add_add_fusion, f32[32,1024]{1,0:T(8,128)S(1)} %fusion.46, bf16[32,2048]{0,1:T(8,128)(2,1)S(1)} %bitcast.64, bf16[2048,1024]{1,0:T(8,128)(2,1)} %bitcast.17), kind=kOutput, calls=%fused_computation.16 | convolution fusion | flops 134316032 | bytes 4653056 | tf_op jit(solution)/shard_map/dot_general | solution.py:127
  (30 shorter events, 1.0 us)
Async XLA Ops:
  0.0 1.6 copy-start
  0.0 5.6 %copy-start.2 = (bf16[32,128]{1,0:T(8,128)(2,1)S(1)}, bf16[32,128]{1,0:T(8,128)(2,1)}, u32[]{:S(2)}) copy-start(bf16[32,128]{1,0:T(8,128)(2,1)} %param.19) | copy-start | bytes 24580
  8.5 11.7 %copy-start.3 = (s32[32,8]{0,1:T(8,128)S(1)}, s32[32,8]{0,1:T(8,128)}, u32[]{:S(2)}) copy-start(s32[32,8]{0,1:T(8,128)} %param.23) | copy-start | bytes 3076
  8.5 12.1 %copy-start.4 = (f32[32,8]{0,1:T(8,128)S(1)}, f32[32,8]{0,1:T(8,128)}, u32[]{:S(2)}) copy-start(f32[32,8]{0,1:T(8,128)} %param.24) | copy-start | bytes 3076
  8.5 12.6 %copy-start.1 = (f32[4096]{0:T(1024)S(1)}, f32[4096]{0:T(1024)}, u32[]{:S(2)}) copy-start(f32[4096]{0:T(1024)} %param.22) | copy-start | bytes 49156
  13.5 7.7 %collective-permute-start = (bf16[32,1024]{1,0:T(8,128)(2,1)S(1)}, bf16[32,1024]{1,0:T(8,128)(2,1)S(1)}, u32[]{:S(2)}, u32[]{:S(2)}) collective-permute-start(bf16[32,1024]{1,0:T(8,128)(2,1)S(1)} %get-tuple-element.9), channel_id=1, source_target_pairs={{0,1},{1,2},{2,3},{3,0},{4,5},{5,6},{6,7},{7,4},{8,9},{9,10},{10,1... | collective-permute-start | bytes 196616 | tf_op jit(solution)/shard_map/ppermute | solution.py:57
  15.6 6.8 %collective-permute-start.1 = (bf16[32,1024]{1,0:T(8,128)(2,1)S(1)}, bf16[32,1024]{1,0:T(8,128)(2,1)S(1)}, u32[]{:S(2)}, u32[]{:S(2)}) collective-permute-start(bf16[32,1024]{1,0:T(8,128)(2,1)S(1)} %get-tuple-element.11), channel_id=1, source_target_pairs={{0,2},{1,3},{2,0},{3,1},{4,6},{5,7},{6,4},{7,5},{8,10},{9,11},{10,... | collective-permute-start | bytes 196616 | tf_op jit(solution)/shard_map/ppermute | solution.py:57
  19.2 4.3 %collective-permute-start.2 = (bf16[32,1024]{1,0:T(8,128)(2,1)S(1)}, bf16[32,1024]{1,0:T(8,128)(2,1)S(1)}, u32[]{:S(2)}, u32[]{:S(2)}) collective-permute-start(bf16[32,1024]{1,0:T(8,128)(2,1)S(1)} %get-tuple-element.10), channel_id=1, source_target_pairs={{0,3},{1,0},{2,1},{3,2},{4,7},{5,4},{6,5},{7,6},{8,11},{9,8},{10,9... | collective-permute-start | bytes 196616 | tf_op jit(solution)/shard_map/ppermute | solution.py:57
  27.4 61.2 %all-to-all-start = ((bf16[128,16,1024]{2,1,0:T(8,128)(2,1)}), bf16[128,16,1024]{2,1,0:T(8,128)(2,1)}, u32[]{:S(2)}, u32[]{:S(2)}) async-start(bf16[128,16,1024]{2,1,0:T(8,128)(2,1)} %bitcast.61), calls=%async_computation | async-start | bytes 8388608 | tf_op jit(solution)/shard_map/all_to_all | solution.py:105
  115.6 57.3 %all-to-all-start.1 = ((bf16[128,16,1024]{2,1,0:T(8,128)(2,1)}), bf16[128,16,1024]{2,1,0:T(8,128)(2,1)}, u32[]{:S(2)}, u32[]{:S(2)}) async-start(bf16[128,16,1024]{2,1,0:T(8,128)(2,1)} %bitcast.62), calls=%async_computation.1 | async-start | bytes 8388608 | tf_op jit(solution)/shard_map/all_to_all | solution.py:120
